TPU v7x, 512 devices: a whole 4x4x16 slice. The times are simulated.
512 devices in a mesh: blk: 8 (over y, core), tiles: 64 (over z, x).
Axes of the slice: x: 4, y: 4, z: 16, core: 2. Of those that a mesh axis runs over, the one named last changes fastest.
Arguments:
- tensor_tiles: bfloat16 [8, 128, 64, 4096], P('blk', 'tiles'), may hold values from -6 to 6
- tile_iblock: int32 [8, 128], P('blk', 'tiles'), may hold values from 0 to 7
- tile_jslot: int32 [8, 128], P('blk', 'tiles'), may hold values from 0 to 1, as said below
- tile_kslot: int32 [8, 128], P('blk', 'tiles'), may hold values from 0 to 1, as said below
- block_jlist: int32 [8, 128], P('blk', 'tiles'), may hold values from 0 to 255, as said below
- block_klist: int32 [8, 128], P('blk', 'tiles'), may hold values from 0 to 63, as said below
- factor_b: bfloat16 [256, 64, 512], P(None, 'tiles'), may hold values from -0.5 to 0.5
- factor_c: bfloat16 [64, 64, 512], P(None, 'tiles'), may hold values from -0.75 to 0.75
Outputs:
- mttkrp: float32 [32768, 512], P(('blk', 'tiles'))
Inputs may be any that keep to these rules, and one draw needn't show every extreme that they name: `block_jlist`: the 2 entries of one device's list are distinct. `block_klist`: the 2 entries of one device's list are distinct. `tile_jslot`: one device's tiles use between 1 and 2 distinct positions, and all 2 on some device. `tile_kslot`: one device's tiles use between 1 and 2 distinct positions, and all 2 on some device.
All inputs are finite; a program needn't handle non-finite values.
Results may differ from a plain program's by a relative error of at most 0.011.
Values may be sent and summed in bfloat16 or wider, within the bound.
A program may use at most 64 MiB of HBM per device.

v0:
```python
import jax
import jax.numpy as jnp
from jax import lax
from jax.sharding import PartitionSpec as P


def outgoing(asked, local, width):
    peers = asked.shape[0] // width
    table = asked.reshape(peers, width).T
    return jnp.take(local, table, axis=0)


def tile_term(local_tiles, which, mode_two, mode_three):
    tile_block = lax.dynamic_index_in_dim(local_tiles, which, 0, keepdims=False)
    inner = tile_block.shape[0]
    across = mode_two.shape[0]
    depth = mode_three.shape[0]
    contracted = jnp.dot(
        tile_block.reshape(inner * across, depth), mode_three, preferred_element_type=jnp.float32
    )
    return jnp.sum(
        contracted.reshape(inner, across, -1) * mode_two.astype(jnp.float32)[None], axis=1
    )


def per_device(
    tensor_tiles, tile_iblock, tile_jslot, tile_kslot, block_jlist, block_klist, factor_b, factor_c
):
    local_tiles = tensor_tiles[0]
    slots_two = tile_jslot[0]
    slots_three = tile_kslot[0]
    count = local_tiles.shape[0]
    wanted_two = jnp.take(block_jlist[0], slots_two)
    wanted_three = jnp.take(block_klist[0], slots_three)
    asked_two, asked_three = (
        lax.all_gather(wanted_two, "tiles", axis=0, tiled=True),
        lax.all_gather(wanted_three, "tiles", axis=0, tiled=True),
    )
    recv_two, recv_three = (
        lax.all_to_all(
            outgoing(asked_two, factor_b, count), "tiles", split_axis=1, concat_axis=2, tiled=True
        ),
        lax.all_to_all(
            outgoing(asked_three, factor_c, count), "tiles", split_axis=1, concat_axis=2, tiled=True
        ),
    )
    pick_two = jnp.arange(count, dtype=jnp.int32)
    pick_three = jnp.arange(count, dtype=jnp.int32)
    rank = factor_b.shape[2]
    fetched_two = recv_two.reshape(count, -1, rank)
    fetched_three = recv_three.reshape(count, -1, rank)
    groups = lax.axis_size("blk")
    inner = local_tiles.shape[1]
    owners = tile_iblock[0]

    def accumulate(which, partial_value):
        mode_two = lax.dynamic_index_in_dim(fetched_two, pick_two[which], 0, keepdims=False)
        mode_three = lax.dynamic_index_in_dim(fetched_three, pick_three[which], 0, keepdims=False)
        term = tile_term(local_tiles, which, mode_two, mode_three)
        target = owners[which]
        current = lax.dynamic_index_in_dim(partial_value, target, 0, keepdims=False)
        return lax.dynamic_update_index_in_dim(partial_value, current + term, target, 0)

    partial_value = lax.fori_loop(
        0, count, accumulate, jnp.zeros((groups, inner, rank), jnp.float32)
    )
    rounded = lax.optimization_barrier(partial_value.astype(jnp.bfloat16)).astype(jnp.float32)
    return lax.psum_scatter(
        rounded.reshape(groups * inner, rank).astype(jnp.bfloat16),
        "blk",
        scatter_dimension=0,
        tiled=True,
    ).astype(jnp.float32)


def solution(mesh):
    placed = (
        P("blk", "tiles", None, None),
        P("blk", "tiles"),
        P("blk", "tiles"),
        P("blk", "tiles"),
        P("blk", "tiles"),
        P("blk", "tiles"),
        P(None, "tiles", None),
        P(None, "tiles", None),
    )
    return jax.shard_map(
        per_device, mesh=mesh, in_specs=placed, out_specs=P(("blk", "tiles"), None), check_vma=False
    )
```

profile of v0, /device:TPU:1, one launch (start us, length us, event | category | flops | bytes accessed | tf_op | source)
XLA Modules:
  0.0 147.0 jit_solution(16779231108427683180)
XLA Ops:
  6.5 0.0 copy-start
  6.5 0.0 copy-start.2
  6.5 0.0 copy-start.3
  6.5 0.7 compare_select_fusion.3
  7.3 0.7 compare_select_fusion.2
  7.9 1.3 dynamic-slice
  9.9 1.3 gather_fusion.2
  11.2 1.3 gather_fusion.3
  12.5 0.0 copy-done.2
  12.5 0.1 fusion.4
  12.5 0.0 copy-done.3
  12.5 0.1 fusion.5
  12.6 29.6 %all-reduce.2 = (s32[128]{0:T(128)S(1)}, s32[128]{0:T(128)S(1)}) all-reduce(s32[128]{0:T(128)S(1)} %fusion.4, s32[128]{0:T(128)S(1)} %fusion.5), channel_id=1, replica_groups=mesh['blk'=8,'tiles'=64] {'tiles'}, use_global_device_ids=true, to_apply=%add | all-reduce | flops 256 | bytes 2048
  42.2 0.1 reshape.69
  42.4 0.1 copy.17
  42.5 0.1 reshape.94
  42.6 0.0 copy-done.1
  42.6 0.9 gather_fusion
  43.4 0.9 broadcast_select_fusion.1
  44.3 7.5 %all-to-all-start = ((bf16[2,64,1,512]{3,0,2,1:T(2,128)(2,1)}), bf16[2,64,1,512]{3,0,2,1:T(2,128)(2,1)S(1)}, u32[]{:S(2)}, u32[]{:S(2)}) async-start(bf16[2,64,1,512]{3,0,2,1:T(2,128)(2,1)} %broadcast_select_fusion.1), calls=%async_computation | async-start | bytes 262144 | tf_op jit(solution)/shard_map/all_to_all | solution.py:43
  51.8 0.1 reshape.71
  51.9 0.1 copy.19
  52.0 0.1 reshape.104
  52.1 0.0 copy-done
  52.1 0.9 gather_fusion.1
  53.0 0.0 copy-start.4
  53.0 0.9 broadcast_select_fusion
  53.9 13.0 %all-to-all-done = bf16[2,64,1,512]{3,0,2,1:T(2,128)(2,1)S(1)} async-done(((bf16[2,64,1,512]{3,0,2,1:T(2,128)(2,1)}), bf16[2,64,1,512]{3,0,2,1:T(2,128)(2,1)S(1)}, u32[]{:S(2)}, u32[]{:S(2)}) %all-to-all-start) | async-done | bytes 131104 | tf_op jit(solution)/shard_map/all_to_all | solution.py:43
  66.9 4.6 %all-to-all-start.1 = ((bf16[2,64,1,512]{3,0,2,1:T(2,128)(2,1)}), bf16[2,64,1,512]{3,0,2,1:T(2,128)(2,1)S(1)}, u32[]{:S(2)}, u32[]{:S(2)}) async-start(bf16[2,64,1,512]{3,0,2,1:T(2,128)(2,1)} %broadcast_select_fusion), calls=%async_computation.1 | async-start | bytes 262144 | tf_op jit(solution)/shard_map/all_to_all | solution.py:40
  71.5 0.0 reduce-scatter.2.cloned.1.call-start
  71.6 15.1 %all-to-all-done.1 = bf16[2,64,1,512]{3,0,2,1:T(2,128)(2,1)S(1)} async-done(((bf16[2,64,1,512]{3,0,2,1:T(2,128)(2,1)}), bf16[2,64,1,512]{3,0,2,1:T(2,128)(2,1)S(1)}, u32[]{:S(2)}, u32[]{:S(2)}) %all-to-all-start.1) | async-done | bytes 131104 | tf_op jit(solution)/shard_map/all_to_all | solution.py:40
  86.7 0.1 broadcast_in_dim.33
  86.8 0.0 copy-done.4
  86.8 16.1 %while.14 = (s32[]{:T(128)}, f32[8,64,512]{2,1,0:T(8,128)S(1)}, s32[2]{0:T(128)S(1)}, bf16[2,64,4096]{2,1,0:T(8,128)(2,1)}, s32[2]{0:T(128)S(1)}, /*index=5*/bf1...) while((s32[]{:T(128)}, f32[8,64,512]{2,1,0:T(8,128)S(1)}, ...), condition=%wide.region_2.4_spmd, body=%wide.region_0.3_spmd.sunk | while | flops 272662528 | bytes 4063449 | solution.py:64
  86.8 0.6 dynamic_slice.71
  89.1 1.1 constant_dynamic-slice_fusion.2
  90.2 1.1 dot_general.7
  91.3 1.3 multiply_reduce_fusion.2
  92.6 0.6 dynamic_slice.70
  94.9 0.6 dynamic_slice.71
  97.2 1.1 constant_dynamic-slice_fusion.2
  98.3 1.1 dot_general.7
  99.4 1.2 multiply_reduce_fusion.2
  100.7 0.6 dynamic_slice.70
  103.0 0.9 convert_element_type.18
  103.8 0.0 reduce-scatter.2.cloned.1.call-update
  103.9 34.8 %reduce-scatter.2.cloned.1.call-done = bf16[64,512]{1,0:T(8,128)(2,1)} async-done(((bf16[512,512]{1,0:T(8,128)(2,1)}), bf16[64,512]{1,0:T(8,128)(2,1)}) %reduce-scatter.2.cloned.1.call-update) | async-done | bytes 65552 | tf_op jit(solution)/shard_map/reduce_scatter | solution.py:68
  138.6 1.5 %convert_element_type.20 = f32[64,512]{1,0:T(8,128)} convert(bf16[64,512]{1,0:T(8,128)(2,1)} %reduce-scatter.2.cloned.1.call-done) | non-fusion elementwise | flops 32768 | bytes 196608 | tf_op jit(solution)/shard_map/convert_element_type | solution.py:73
  (18 shorter events, 0.2 us)
Async XLA Ops:
  6.5 45.6 %copy-start = (bf16[256,1,512]{2,0,1:T(8,128)(2,1)S(1)}, bf16[256,1,512]{2,0,1:T(8,128)(2,1)}, u32[]{:S(2)}) copy-start(bf16[256,1,512]{2,0,1:T(8,128)(2,1)} %param.18) | copy-start | bytes 786436
  6.5 5.9 %copy-start.2 = (s32[1,2]{1,0:T(1,128)S(1)}, s32[1,2]{1,0:T(1,128)}, u32[]{:S(2)}) copy-start(s32[1,2]{1,0:T(1,128)} %param.15) | copy-start | bytes 28
  6.5 6.0 %copy-start.3 = (s32[1,2]{1,0:T(1,128)S(1)}, s32[1,2]{1,0:T(1,128)}, u32[]{:S(2)}) copy-start(s32[1,2]{1,0:T(1,128)} %param.14) | copy-start | bytes 28
  6.5 36.0 %copy-start.1 = (bf16[64,1,512]{2,0,1:T(8,128)(2,1)S(1)}, bf16[64,1,512]{2,0,1:T(8,128)(2,1)}, u32[]{:S(2)}) copy-start(bf16[64,1,512]{2,0,1:T(8,128)(2,1)} %param.19) | copy-start | bytes 196612
  44.3 22.6 %all-to-all-start = ((bf16[2,64,1,512]{3,0,2,1:T(2,128)(2,1)}), bf16[2,64,1,512]{3,0,2,1:T(2,128)(2,1)S(1)}, u32[]{:S(2)}, u32[]{:S(2)}) async-start(bf16[2,64,1,512]{3,0,2,1:T(2,128)(2,1)} %broadcast_select_fusion.1), calls=%async_computation | async-start | bytes 262144 | tf_op jit(solution)/shard_map/all_to_all | solution.py:43
  53.0 33.8 %copy-start.4 = (s32[1,2]{1,0:T(1,128)S(1)}, s32[1,2]{1,0:T(1,128)}, u32[]{:S(2)}) copy-start(s32[1,2]{1,0:T(1,128)} %param.13) | copy-start | bytes 28
  66.9 19.8 %all-to-all-start.1 = ((bf16[2,64,1,512]{3,0,2,1:T(2,128)(2,1)}), bf16[2,64,1,512]{3,0,2,1:T(2,128)(2,1)S(1)}, u32[]{:S(2)}, u32[]{:S(2)}) async-start(bf16[2,64,1,512]{3,0,2,1:T(2,128)(2,1)} %broadcast_select_fusion), calls=%async_computation.1 | async-start | bytes 262144 | tf_op jit(solution)/shard_map/all_to_all | solution.py:40
  71.5 67.1 %reduce-scatter.2.cloned.1.call-start = ((), (), s32[]{:S(2)}) async-start(), calls=%async_computation.3 | async-start | bytes 589824 | tf_op jit(solution)/shard_map/reduce_scatter | solution.py:68
Sparse Core Ops, SparseCore 0:
  104.0 34.6 reduce-scatter.1
where the time goes:
time: 148 us; the launch traced here: 147 us
  waiting for transfers between devices  62.9 us (42%)
  blocking collectives  29.6 us (20%)
  between operations  14.2 us (10%)
  local copies, waits for them, and re-layouts  13 us (9%)
  starting transfers between devices  12.1 us (8%)
  loops' own time  6.83 us (5%)
  other arithmetic  5.82 us (4%)
  matrix products  2.49 us (2%)
    reduce_scatter x1, waiting for transfers between devices, per_device(): lax.psum_scatter(rounded.reshape(groups * inner, rank).astype(jnp.bfloat1...  34.8 us
    unnamed x1, blocking collectives  29.6 us
    all_to_all x1, waiting for transfers between devices, per_device(): lax.all_to_all(outgoing(asked_two, factor_b, count), 'tiles', split_axis=...  15.1 us
    all_to_all x1, waiting for transfers between devices, per_device(): lax.all_to_all(outgoing(asked_three, factor_c, count), 'tiles', split_axi...  13 us
    all_to_all x1, starting transfers between devices, per_device(): lax.all_to_all(outgoing(asked_three, factor_c, count), 'tiles', split_axi...  7.47 us
    another operation x1, loops' own time, per_device(): lax.fori_loop(0, count, accumulate, jnp.zeros((groups, inner, rank), jnp....  6.83 us
    all_to_all x1, starting transfers between devices, per_device(): lax.all_to_all(outgoing(asked_two, factor_b, count), 'tiles', split_axis=...  4.62 us
  transfers between devices with their start and end apart: 3, of which 3 were waited for; matrix products, arithmetic and copies ran while one was open for 1% of the time, Pallas kernels for 0%

commit v1 on v0

v1 whole, which is shorter than its diff:
```python
import functools

import jax
import jax.numpy as jnp
from jax import lax
from jax.experimental import pallas as pl
from jax.experimental.pallas import tpu as pltpu
from jax.sharding import PartitionSpec as P

MESH = pl.DeviceIdType.MESH
F32 = jnp.float32
BF16 = jnp.bfloat16
LANES = 128
STAGE = 9


def one_hot(mask):
    return jnp.where(mask, 1.0, 0.0).astype(F32).astype(BF16)


def wait_bytes(ref, sem):
    pltpu.make_async_copy(ref, ref, sem).wait()


def kernel(
    groups, peers,
    tiles_hbm, iblock_hbm, jslot_hbm, kslot_hbm, jlist_hbm, klist_hbm, two_hbm, three_hbm,
    out_ref,
    iblock, jslot, kslot, jlist, klist, tiles, two, three,
    asked, mine, order, send_two, send_three, recv_two, recv_three, rows_two, rows_three,
    send_part, recv_part,
    local_sem, asked_sem, three_sem, two_sem, part_sem,
):
    count, inner, flat = tiles.shape
    rank = two.shape[1]
    across = peers
    chunks = rank // LANES
    slab = count * chunks
    me = lax.axis_index("tiles")
    row = lax.axis_index("blk")

    pairs = (
        (iblock_hbm, iblock), (jslot_hbm, jslot), (kslot_hbm, kslot), (jlist_hbm, jlist),
        (klist_hbm, klist), (three_hbm, three), (two_hbm, two), (tiles_hbm, tiles),
    )
    loads = [
        pltpu.make_async_copy(source, target, local_sem.at[index])
        for index, (source, target) in enumerate(pairs)
    ]
    for load in loads:
        load.start()

    barrier = pltpu.get_barrier_semaphore()

    def greet(step, carry):
        other = lax.rem(me + step, peers)
        pl.semaphore_signal(barrier, inc=1, device_id={"tiles": other}, device_id_type=MESH)
        return carry

    lax.fori_loop(1, peers, greet, 0)
    for step in range(1, groups):
        other = lax.rem(row + step, groups)
        pl.semaphore_signal(barrier, inc=1, device_id={"blk": other}, device_id_type=MESH)

    wide = peers * slab
    place = lax.broadcasted_iota(jnp.int32, (wide, wide), 0)
    column = lax.broadcasted_iota(jnp.int32, (wide, wide), 1)
    order[...] = one_hot(column == (place % peers) * slab + place // peers)

    for load in loads[:5]:
        load.wait()
    words = [
        jlist[0, jslot[0, which]] + klist[0, kslot[0, which]] * 65536 for which in range(count)
    ]
    lane = lax.broadcasted_iota(jnp.int32, (1, LANES), 1)
    message = jnp.where(lane < LANES // 2, words[0], words[1])
    mine[...] = message
    asked[pl.ds(me, 1)] = message.reshape(1, 1, LANES)

    pl.semaphore_wait(barrier, peers - 1 + groups - 1)
    if STAGE < 2:
        for load in loads[5:]:
            load.wait()
        out_ref[...] = jnp.zeros_like(out_ref)
        return

    def ask(step, carry):
        other = lax.rem(me + step, peers)
        pltpu.make_async_remote_copy(
            mine, asked.at[me], asked_sem.at[0], asked_sem.at[1],
            device_id={"tiles": other}, device_id_type=MESH,
        ).start()
        return carry

    lax.fori_loop(1, peers, ask, 0)
    for load in loads[5:7]:
        load.wait()
    wait_bytes(asked.at[pl.ds(0, peers - 1)], asked_sem.at[1])
    if STAGE < 3:
        wait_bytes(asked.at[pl.ds(0, peers - 1)], asked_sem.at[0])
        loads[7].wait()
        out_ref[...] = jnp.zeros_like(out_ref)
        return

    given = jnp.broadcast_to(asked[...], (peers, slab, LANES))
    turned = pltpu.roll(given.reshape(wide, LANES), LANES // 2, 1).reshape(peers, slab, LANES)
    sub = lax.broadcasted_iota(jnp.int32, (peers, slab, LANES), 1)
    lane = lax.broadcasted_iota(jnp.int32, (peers, slab, LANES), 2)
    word = jnp.where((sub < chunks) == (lane < LANES // 2), given, turned).reshape(wide, LANES)
    chunk = lax.broadcasted_iota(jnp.int32, (wide, LANES), 0) % chunks
    lane = lax.broadcasted_iota(jnp.int32, (wide, LANES), 1)

    def select(wanted, table):
        total = table.shape[0]
        key = wanted + chunk * total
        stacked = jnp.concatenate(
            [table[:, c * LANES : (c + 1) * LANES] for c in range(chunks)], axis=0
        )
        hot = jnp.concatenate(
            [one_hot(key == lane + start) for start in range(0, chunks * total, LANES)], axis=1
        )
        return jnp.dot(hot, stacked, preferred_element_type=F32).astype(BF16)

    def hand_out(send, recv, sem):
        def give(step, carry):
            other = lax.rem(me + step, peers)
            pltpu.make_async_remote_copy(
                send.at[other], recv.at[me], sem.at[0], sem.at[1],
                device_id={"tiles": other}, device_id_type=MESH,
            ).start()
            return carry

        lax.fori_loop(1, peers, give, 0)
        recv[pl.ds(me, 1)] = send[pl.ds(me, 1)]

    send_three[...] = select(lax.shift_right_logical(word, 16), three).reshape(peers, slab, LANES)
    if STAGE >= 4:
        hand_out(send_three, recv_three, three_sem)
    send_two[...] = select(lax.bitwise_and(word, 65535), two).reshape(peers, slab, LANES)
    if STAGE >= 4:
        hand_out(send_two, recv_two, two_sem)
    wait_bytes(asked.at[pl.ds(0, peers - 1)], asked_sem.at[0])
    loads[7].wait()
    if STAGE < 4:
        out_ref[...] = jnp.zeros_like(out_ref)
        return

    def arrange(recv, rows):
        sorted_rows = jnp.dot(
            order[...], recv[...].reshape(wide, LANES), preferred_element_type=F32
        )
        for which in range(count):
            for c in range(chunks):
                start = (which * chunks + c) * peers
                rows[which, :, c * LANES : (c + 1) * LANES] = sorted_rows[start : start + peers]

    some = pl.ds(0, peers - 1)
    wait_bytes(recv_three.at[some], three_sem.at[1])
    arrange(recv_three, rows_three)
    wait_bytes(recv_two.at[some], two_sem.at[1])
    arrange(recv_two, rows_two)
    wait_bytes(recv_three.at[some], three_sem.at[0])
    wait_bytes(recv_two.at[some], two_sem.at[0])
    if STAGE < 5:
        out_ref[...] = jnp.zeros_like(out_ref)
        return

    half = rank // 2
    together = 4
    depth = flat // across
    for part in range(2):
        columns = slice(part * half, (part + 1) * half)
        terms = []
        for which in range(count):
            mode_three = rows_three[which, :, columns]
            term = jnp.zeros((inner, half), F32)
            for first in range(0, across, together):
                product = jnp.concatenate(
                    [
                        (mode_three * rows_two[which, j : j + 1, columns]).astype(BF16)
                        for j in range(first, first + together)
                    ],
                    axis=0,
                )
                left = tiles[which, :, first * depth : (first + together) * depth]
                term = term + jnp.dot(left, product, preferred_element_type=F32)
            terms.append(term)
        for group in range(groups):
            total = jnp.zeros((inner, half), F32)
            for which in range(count):
                total = total + jnp.where(iblock[0, which] == group, terms[which], 0.0)
            send_part[part, group] = total.astype(BF16)
        if STAGE >= 6:
            for step in range(1, groups):
                other = lax.rem(row + step, groups)
                pltpu.make_async_remote_copy(
                    send_part.at[part, other], recv_part.at[part, row],
                    part_sem.at[0, part], part_sem.at[1, part],
                    device_id={"blk": other}, device_id_type=MESH,
                ).start()
            recv_part[part, pl.ds(row, 1)] = send_part[part, pl.ds(row, 1)]
    if STAGE < 6:
        out_ref[...] = jnp.concatenate([send_part[0, 0], send_part[1, 0]], axis=1).astype(F32)
        return

    for part in range(2):
        wait_bytes(recv_part.at[part, pl.ds(0, groups - 1)], part_sem.at[1, part])
        total = recv_part[part, 0].astype(F32)
        for group in range(1, groups):
            total = total + recv_part[part, group].astype(F32)
        out_ref[:, part * half : (part + 1) * half] = total
    for part in range(2):
        wait_bytes(send_part.at[part, pl.ds(0, groups - 1)], part_sem.at[0, part])


def per_device(
    tensor_tiles, tile_iblock, tile_jslot, tile_kslot, block_jlist, block_klist, factor_b, factor_c
):
    groups = lax.axis_size("blk")
    peers = lax.axis_size("tiles")
    tiles = tensor_tiles[0]
    two = factor_b.reshape(factor_b.shape[0], factor_b.shape[2])
    three = factor_c.reshape(factor_c.shape[0], factor_c.shape[2])
    count, inner, _ = tiles.shape
    rank = two.shape[1]
    slab = count * rank // LANES
    wide = peers * slab
    any_space = pl.BlockSpec(memory_space=pl.ANY)
    dma = pltpu.SemaphoreType.DMA
    rows = pltpu.VMEM((peers, slab, LANES), BF16)
    return pl.pallas_call(
        functools.partial(kernel, groups, peers),
        out_shape=jax.ShapeDtypeStruct((inner, rank), F32),
        in_specs=[any_space] * 8,
        out_specs=pl.BlockSpec(memory_space=pltpu.VMEM),
        scratch_shapes=[
            *[pltpu.SMEM((1, count), jnp.int32)] * 5,
            pltpu.VMEM(tiles.shape, BF16),
            pltpu.VMEM(two.shape, BF16),
            pltpu.VMEM(three.shape, BF16),
            pltpu.VMEM((peers, 1, LANES), jnp.int32),
            pltpu.VMEM((1, LANES), jnp.int32),
            pltpu.VMEM((wide, wide), BF16),
            rows, rows, rows, rows,
            pltpu.VMEM((count, peers, rank), F32),
            pltpu.VMEM((count, peers, rank), F32),
            pltpu.VMEM((2, groups, inner, rank // 2), BF16),
            pltpu.VMEM((2, groups, inner, rank // 2), BF16),
            dma((8,)), dma((2,)), dma((2,)), dma((2,)), dma((2, 2)),
        ],
        compiler_params=pltpu.CompilerParams(
            collective_id=0, has_side_effects=True, vmem_limit_bytes=40 * 1024 * 1024
        ),
    )(tiles, tile_iblock, tile_jslot, tile_kslot, block_jlist, block_klist, two, three)


def solution(mesh):
    placed = (
        P("blk", "tiles", None, None),
        P("blk", "tiles"),
        P("blk", "tiles"),
        P("blk", "tiles"),
        P("blk", "tiles"),
        P("blk", "tiles"),
        P(None, "tiles", None),
        P(None, "tiles", None),
    )
    return jax.shard_map(
        per_device, mesh=mesh, in_specs=placed, out_specs=P(("blk", "tiles"), None), check_vma=False
    )
```

time: 148 us -> 58.4 us (0.39)
  waiting for transfers between devices: 62.9 us -> 0 us
  Pallas kernels: 0 us -> 53.7 us
  blocking collectives: 29.6 us -> 0 us
  between operations: 14.2 us -> 0.03 us
  starting transfers between devices: 12.1 us -> 0 us
  local copies, waits for them, and re-layouts: 13 us -> 4.37 us
  loops' own time: 6.83 us -> 0 us
  other arithmetic: 5.82 us -> 0 us
  matrix products: 2.49 us -> 0 us
    pallas_call x0 -> x1, Pallas kernels: none -> 53.7 us  [per_device(): pl.pallas_call(functools.partial(kernel, groups, peers), out_shape=jax.Sh...]
    reduce_scatter x1 -> x0, waiting for transfers between devices: 34.8 us -> none  [per_device(): lax.psum_scatter(rounded.reshape(groups * inner, rank).astype(jnp.bfloat1...]
    unnamed x1 -> x0, blocking collectives: 29.6 us -> none
    all_to_all x2 -> x0, waiting for transfers between devices: 28.1 us -> none  [the longest x1 15.1 us: per_device(): lax.all_to_all(outgoing(asked_two, factor_b, count), 'tiles', split_axis=...]
    all_to_all x2 -> x0, starting transfers between devices: 12.1 us -> none  [the longest x1 7.47 us: per_device(): lax.all_to_all(outgoing(asked_three, factor_c, count), 'tiles', split_axi...]
    another operation x1 -> x0, loops' own time: 6.83 us -> none  [per_device(): lax.fori_loop(0, count, accumulate, jnp.zeros((groups, inner, rank), jnp....]
    dynamic_slice x6 -> x0, local copies, waits for them, and re-layouts: 4.49 us -> none  [the longest x2 2.16 us: tile_term(): tile_block = lax.dynamic_index_in_dim(local_tiles, which, 0, keepdims=False)]
    gather x4 -> x0, local copies, waits for them, and re-layouts: 4.29 us -> none  [the longest x2 1.7 us: outgoing(): return jnp.take(local, table, axis=0)]
  transfers between devices with their start and end apart: 3 -> 0, of which waited for: 3 -> 0; matrix products, arithmetic and copies ran while one was open for 1% -> 0% of each run, Pallas kernels for 0% -> 0%
where the time goes in v1:
time: 58.4 us; the launch traced here: 58.1 us
  Pallas kernels  53.7 us (92%)
  local copies, waits for them, and re-layouts  4.37 us (7%)
    pallas_call x1, Pallas kernels, per_device(): pl.pallas_call(functools.partial(kernel, groups, peers), out_shape=jax.Sh...  53.7 us
    unnamed x17, local copies, waits for them, and re-layouts  4.37 us

profile of v1, /device:TPU:1, one launch (start us, length us, event | category | flops | bytes accessed | tf_op | source)
XLA Modules:
  0.0 58.1 jit_solution(6253772334511185322)
XLA Ops:
  0.0 0.0 copy-start.6
  0.0 0.0 copy-start.7
  0.0 0.0 copy-start.3
  0.0 0.0 copy-start.4
  0.0 0.0 copy-start.5
  0.0 0.6 %copy-done.6 = s32[1,2]{1,0:T(1,128)S(1)} copy-done((s32[1,2]{1,0:T(1,128)S(1)}, s32[1,2]{1,0:T(1,128)}, u32[]{:S(2)}) %copy-start.6) | copy-done | bytes 32
  0.7 0.0 copy-done.7
  0.7 0.0 copy-done.3
  0.7 0.0 copy-done.4
  0.7 0.0 copy-done.5
  0.7 0.0 copy-start
  0.7 1.2 %copy-done = bf16[1,2,64,4096]{3,2,1,0:T(8,128)(2,1)S(1)} copy-done((bf16[1,2,64,4096]{3,2,1,0:T(8,128)(2,1)S(1)}, bf16[1,2,64,4096]{3,2,1,0:T(8,128)(2,1)}, u32[]{:S(2)}) %copy-start) | copy-done | bytes 1048600
  1.9 0.0 copy-start.1
  1.9 0.9 %copy-done.1 = bf16[256,1,512]{2,0,1:T(8,128)(2,1)S(1)} copy-done((bf16[256,1,512]{2,0,1:T(8,128)(2,1)S(1)}, bf16[256,1,512]{2,0,1:T(8,128)(2,1)}, u32[]{:S(2)}) %copy-start.1) | copy-done | bytes 262168
  2.9 0.0 copy-start.2
  2.9 0.8 %copy-done.2 = bf16[64,1,512]{2,0,1:T(8,128)(2,1)S(1)} copy-done((bf16[64,1,512]{2,0,1:T(8,128)(2,1)S(1)}, bf16[64,1,512]{2,0,1:T(8,128)(2,1)}, u32[]{:S(2)}) %copy-start.2) | copy-done | bytes 65560
  3.7 53.7 %shard_map.82 = f32[64,512]{1,0:T(8,128)S(1)} custom-call(bf16[2,64,4096]{2,1,0:T(8,128)(2,1)S(1)} %bitcast.3, s32[1,2]{1,0:T(1,128)S(1)} %copy-done.3, s32[1,2]{1,0:T(1,128)S(1)} %copy-done.4, s32[1,2]{1,0:T(1,128)S(1)} %copy-done.5, s32[1,2]{1,0:T(1,128)S(1)} %copy-done.6, s32[1,2]{1,0:T(1,128)S(1)} %copy-done.7, bf16[256,512]{1,0:T(8,128)(2,1)S(1)} %bitcast.4, ...), custom_call_target="tpu_custom_call" | custom-call | tf_op jit(solution)/shard_map/pallas_call | solution.py:231
  57.5 0.7 %copy.10 = f32[64,512]{1,0:T(8,128)} copy(f32[64,512]{1,0:T(8,128)S(1)} %shard_map.82) | data formatting | bytes 262144
Async XLA Ops:
  0.0 0.7 %copy-start.6 = (s32[1,2]{1,0:T(1,128)S(1)}, s32[1,2]{1,0:T(1,128)}, u32[]{:S(2)}) copy-start(s32[1,2]{1,0:T(1,128)} %jlist_hbm.1) | copy-start | bytes 28
  0.0 0.7 %copy-start.7 = (s32[1,2]{1,0:T(1,128)S(1)}, s32[1,2]{1,0:T(1,128)}, u32[]{:S(2)}) copy-start(s32[1,2]{1,0:T(1,128)} %klist_hbm.1) | copy-start | bytes 28
  0.0 0.7 %copy-start.3 = (s32[1,2]{1,0:T(1,128)S(1)}, s32[1,2]{1,0:T(1,128)}, u32[]{:S(2)}) copy-start(s32[1,2]{1,0:T(1,128)} %iblock_hbm.1) | copy-start | bytes 28
  0.0 0.7 %copy-start.4 = (s32[1,2]{1,0:T(1,128)S(1)}, s32[1,2]{1,0:T(1,128)}, u32[]{:S(2)}) copy-start(s32[1,2]{1,0:T(1,128)} %jslot_hbm.1) | copy-start | bytes 28
  0.0 0.7 %copy-start.5 = (s32[1,2]{1,0:T(1,128)S(1)}, s32[1,2]{1,0:T(1,128)}, u32[]{:S(2)}) copy-start(s32[1,2]{1,0:T(1,128)} %kslot_hbm.1) | copy-start | bytes 28
  0.7 1.2 %copy-start = (bf16[1,2,64,4096]{3,2,1,0:T(8,128)(2,1)S(1)}, bf16[1,2,64,4096]{3,2,1,0:T(8,128)(2,1)}, u32[]{:S(2)}) copy-start(bf16[1,2,64,4096]{3,2,1,0:T(8,128)(2,1)} %param.8) | copy-start | bytes 3145732
  1.9 0.9 %copy-start.1 = (bf16[256,1,512]{2,0,1:T(8,128)(2,1)S(1)}, bf16[256,1,512]{2,0,1:T(8,128)(2,1)}, u32[]{:S(2)}) copy-start(bf16[256,1,512]{2,0,1:T(8,128)(2,1)} %param.14) | copy-start | bytes 786436
  2.9 0.8 %copy-start.2 = (bf16[64,1,512]{2,0,1:T(8,128)(2,1)S(1)}, bf16[64,1,512]{2,0,1:T(8,128)(2,1)}, u32[]{:S(2)}) copy-start(bf16[64,1,512]{2,0,1:T(8,128)(2,1)} %param.15) | copy-start | bytes 196612

commit v2 on v1

--- a/solution.py
+++ b/solution.py
@@ -12,6 +12,9 @@
 BF16 = jnp.bfloat16
 LANES = 128
 STAGE = 9
+EARLY = 4
+SIDE = 4
+REACH = 4
 
 
 def one_hot(mask):
@@ -20,6 +23,46 @@
 
 def wait_bytes(ref, sem):
     pltpu.make_async_copy(ref, ref, sem).wait()
+
+
+def spread(me, peers, visit):
+    lanes = SIDE
+    planes = peers // lanes
+
+    def body(step, carry):
+        turn, side = step // lanes, step % lanes
+        away = (turn + 1) // 2
+        far = planes // 2 + jnp.where(turn % 2 == 0, away, -away)
+        plane = lax.rem(me // lanes + far, planes)
+        other = plane * lanes + lax.rem(me + side, lanes)
+
+        @pl.when(other != me)
+        def _():
+            visit(other)
+
+        return carry
+
+    lax.fori_loop(0, peers, body, 0)
+
+
+def spread_early(me, peers, visit):
+    early = EARLY * SIDE
+
+    def body(other, carry):
+        @pl.when(other != me)
+        def _():
+            visit(other)
+
+        return carry
+
+    lax.fori_loop(0, early, body, 0)
+
+    def rest(other):
+        @pl.when(other >= early)
+        def _():
+            visit(other)
+
+    spread(me, peers, rest)
 
 
 def kernel(
@@ -27,9 +70,9 @@
     tiles_hbm, iblock_hbm, jslot_hbm, kslot_hbm, jlist_hbm, klist_hbm, two_hbm, three_hbm,
     out_ref,
     iblock, jslot, kslot, jlist, klist, tiles, two, three,
-    asked, mine, order, send_two, send_three, recv_two, recv_three, rows_two, rows_three,
+    asked, order, send, recv, rows_two, rows_three,
     send_part, recv_part,
-    local_sem, asked_sem, three_sem, two_sem, part_sem,
+    local_sem, asked_sem, near_sem, rows_sem, part_sem,
 ):
     count, inner, flat = tiles.shape
     rank = two.shape[1]
@@ -52,12 +95,26 @@
 
     barrier = pltpu.get_barrier_semaphore()
 
-    def greet(step, carry):
-        other = lax.rem(me + step, peers)
-        pl.semaphore_signal(barrier, inc=1, device_id={"tiles": other}, device_id_type=MESH)
-        return carry
-
-    lax.fori_loop(1, peers, greet, 0)
+    planes = peers // SIDE
+    plane, lane_x = me // SIDE, lax.rem(me, SIDE)
+    offsets = [sign * away for away in range(REACH, 0, -1) for sign in (1, -1)]
+
+    def along(offset):
+        return lax.rem(plane + (offset + planes), planes)
+
+    def at_plane(offset):
+        return {"tiles": along(offset) * SIDE + lane_x}
+
+    def at_lane(step):
+        return {"tiles": plane * SIDE + lax.rem(lane_x + step, SIDE)}
+
+    def entry(offset):
+        return asked.at[pl.ds(lane_x * planes + along(offset), 1)]
+
+    for offset in offsets:
+        pl.semaphore_signal(barrier, inc=1, device_id=at_plane(offset), device_id_type=MESH)
+    for step in (2, 1, 3):
+        pl.semaphore_signal(barrier, inc=1, device_id=at_lane(step), device_id_type=MESH)
     for step in range(1, groups):
         other = lax.rem(row + step, groups)
         pl.semaphore_signal(barrier, inc=1, device_id={"blk": other}, device_id_type=MESH)
@@ -74,28 +131,34 @@
     ]
     lane = lax.broadcasted_iota(jnp.int32, (1, LANES), 1)
     message = jnp.where(lane < LANES // 2, words[0], words[1])
-    mine[...] = message
-    asked[pl.ds(me, 1)] = message.reshape(1, 1, LANES)
-
-    pl.semaphore_wait(barrier, peers - 1 + groups - 1)
+    asked[pl.ds(lane_x * planes + plane, 1)] = message.reshape(1, 1, LANES)
+
+    pl.semaphore_wait(barrier, 2 * REACH + SIDE - 1 + groups - 1)
     if STAGE < 2:
         for load in loads[5:]:
             load.wait()
         out_ref[...] = jnp.zeros_like(out_ref)
         return
 
-    def ask(step, carry):
-        other = lax.rem(me + step, peers)
+    def pass_on(what, sem, target):
         pltpu.make_async_remote_copy(
-            mine, asked.at[me], asked_sem.at[0], asked_sem.at[1],
-            device_id={"tiles": other}, device_id_type=MESH,
+            what, what, asked_sem.at[0], sem, device_id=target, device_id_type=MESH
         ).start()
-        return carry
-
-    lax.fori_loop(1, peers, ask, 0)
+
+    for offset in offsets:
+        pass_on(entry(0), near_sem.at[offset + REACH], at_plane(offset))
+    for offset in offsets:
+        wait_bytes(entry(-offset), near_sem.at[offset + REACH])
+        if offset < 0:
+            pass_on(entry(-offset), asked_sem.at[1], at_plane(-REACH))
+        elif offset < REACH:
+            pass_on(entry(-offset), asked_sem.at[1], at_plane(REACH))
+    wait_bytes(asked.at[pl.ds(0, 2 * REACH - 1)], asked_sem.at[1])
+    for step in (2, 1, 3):
+        pass_on(asked.at[pl.ds(lane_x * planes, planes)], asked_sem.at[2], at_lane(step))
     for load in loads[5:7]:
         load.wait()
-    wait_bytes(asked.at[pl.ds(0, peers - 1)], asked_sem.at[1])
+    wait_bytes(asked.at[pl.ds(0, peers - planes)], asked_sem.at[2])
     if STAGE < 3:
         wait_bytes(asked.at[pl.ds(0, peers - 1)], asked_sem.at[0])
         loads[7].wait()
@@ -121,33 +184,27 @@
         )
         return jnp.dot(hot, stacked, preferred_element_type=F32).astype(BF16)
 
-    def hand_out(send, recv, sem):
-        def give(step, carry):
-            other = lax.rem(me + step, peers)
-            pltpu.make_async_remote_copy(
-                send.at[other], recv.at[me], sem.at[0], sem.at[1],
-                device_id={"tiles": other}, device_id_type=MESH,
-            ).start()
-            return carry
-
-        lax.fori_loop(1, peers, give, 0)
-        recv[pl.ds(me, 1)] = send[pl.ds(me, 1)]
-
-    send_three[...] = select(lax.shift_right_logical(word, 16), three).reshape(peers, slab, LANES)
+    send[:, 0] = select(lax.shift_right_logical(word, 16), three).reshape(peers, slab, LANES)
+    send[:, 1] = select(lax.bitwise_and(word, 65535), two).reshape(peers, slab, LANES)
+
+    def give(other):
+        pltpu.make_async_remote_copy(
+            send.at[lax.rem(other, SIDE) * planes + other // SIDE], recv.at[me], rows_sem.at[0], rows_sem.at[1],
+            device_id={"tiles": other}, device_id_type=MESH,
+        ).start()
+
     if STAGE >= 4:
-        hand_out(send_three, recv_three, three_sem)
-    send_two[...] = select(lax.bitwise_and(word, 65535), two).reshape(peers, slab, LANES)
-    if STAGE >= 4:
-        hand_out(send_two, recv_two, two_sem)
+        spread_early(me, peers, give)
+        recv[pl.ds(me, 1)] = send[pl.ds(lane_x * planes + plane, 1)]
     wait_bytes(asked.at[pl.ds(0, peers - 1)], asked_sem.at[0])
     loads[7].wait()
     if STAGE < 4:
         out_ref[...] = jnp.zeros_like(out_ref)
         return
 
-    def arrange(recv, rows):
+    def arrange(part, rows):
         sorted_rows = jnp.dot(
-            order[...], recv[...].reshape(wide, LANES), preferred_element_type=F32
+            order[...], recv[:, part].reshape(wide, LANES), preferred_element_type=F32
         )
         for which in range(count):
             for c in range(chunks):
@@ -155,12 +212,10 @@
                 rows[which, :, c * LANES : (c + 1) * LANES] = sorted_rows[start : start + peers]
 
     some = pl.ds(0, peers - 1)
-    wait_bytes(recv_three.at[some], three_sem.at[1])
-    arrange(recv_three, rows_three)
-    wait_bytes(recv_two.at[some], two_sem.at[1])
-    arrange(recv_two, rows_two)
-    wait_bytes(recv_three.at[some], three_sem.at[0])
-    wait_bytes(recv_two.at[some], two_sem.at[0])
+    wait_bytes(recv.at[some], rows_sem.at[1])
+    arrange(0, rows_three)
+    arrange(1, rows_two)
+    wait_bytes(send.at[some], rows_sem.at[0])
     if STAGE < 5:
         out_ref[...] = jnp.zeros_like(out_ref)
         return
@@ -227,7 +282,7 @@
     wide = peers * slab
     any_space = pl.BlockSpec(memory_space=pl.ANY)
     dma = pltpu.SemaphoreType.DMA
-    rows = pltpu.VMEM((peers, slab, LANES), BF16)
+    rows = pltpu.VMEM((peers, 2, slab, LANES), BF16)
     return pl.pallas_call(
         functools.partial(kernel, groups, peers),
         out_shape=jax.ShapeDtypeStruct((inner, rank), F32),
@@ -239,17 +294,16 @@
             pltpu.VMEM(two.shape, BF16),
             pltpu.VMEM(three.shape, BF16),
             pltpu.VMEM((peers, 1, LANES), jnp.int32),
-            pltpu.VMEM((1, LANES), jnp.int32),
             pltpu.VMEM((wide, wide), BF16),
-            rows, rows, rows, rows,
+            rows, rows,
             pltpu.VMEM((count, peers, rank), F32),
             pltpu.VMEM((count, peers, rank), F32),
             pltpu.VMEM((2, groups, inner, rank // 2), BF16),
             pltpu.VMEM((2, groups, inner, rank // 2), BF16),
-            dma((8,)), dma((2,)), dma((2,)), dma((2,)), dma((2, 2)),
+            dma((8,)), dma((3,)), dma((2 * REACH + 1,)), dma((2,)), dma((2, 2)),
         ],
         compiler_params=pltpu.CompilerParams(
-            collective_id=0, has_side_effects=True, vmem_limit_bytes=40 * 1024 * 1024
+            collective_id=0, has_side_effects=True
         ),
     )(tiles, tile_iblock, tile_jslot, tile_kslot, block_jlist, block_klist, two, three)
 

time: 58.4 us -> 48.1 us (0.82)
  Pallas kernels: 53.7 us -> 45.8 us
  local copies, waits for them, and re-layouts: 4.37 us -> 1.57 us
    pallas_call x1, Pallas kernels: 53.7 us -> 45.8 us  [per_device(): pl.pallas_call(functools.partial(kernel, groups, peers), out_shape=jax.Sh...]
    unnamed x17 -> x1, local copies, waits for them, and re-layouts: 4.37 us -> 1.57 us
where the time goes in v2:
time: 48.1 us; the launch traced here: 47.4 us
  Pallas kernels  45.8 us (95%)
  local copies, waits for them, and re-layouts  1.57 us (3%)
    pallas_call x1, Pallas kernels, per_device(): pl.pallas_call(functools.partial(kernel, groups, peers), out_shape=jax.Sh...  45.8 us
    unnamed x1, local copies, waits for them, and re-layouts  1.57 us

profile of v2, /device:TPU:1, one launch (start us, length us, event | category | flops | bytes accessed | tf_op | source)
XLA Modules:
  0.0 47.4 jit_solution(12624437650389344497)
XLA Ops:
  0.0 45.8 %shard_map.82 = f32[64,512]{1,0:T(8,128)} custom-call(bf16[2,64,4096]{2,1,0:T(8,128)(2,1)} %bitcast.3, s32[1,2]{1,0:T(1,128)} %iblock_hbm.1, s32[1,2]{1,0:T(1,128)} %jslot_hbm.1, s32[1,2]{1,0:T(1,128)} %kslot_hbm.1, s32[1,2]{1,0:T(1,128)} %jlist_hbm.1, s32[1,2]{1,0:T(1,128)} %klist_hbm.1, bf16[256,512]{1,0:T(8,128)(2,1)} %bitcast.4, bf16[64,512]{1,0:T(8,128)(2,1)} %bitcast.5), custom_call_target="tpu_custom_call" | custom-call | tf_op jit(solution)/shard_map/pallas_call | solution.py:286
  45.8 1.6 %copy.10 = f32[64,512]{1,0:T(8,128)} copy(f32[64,512]{1,0:T(8,128)} %shard_map.82) | data formatting | bytes 262144

commit v3 on v0

v3 whole, which is shorter than its diff:
```python
import functools

import jax
import jax.numpy as jnp
from jax import lax
from jax.experimental import pallas as pl
from jax.experimental.pallas import tpu as pltpu
from jax.sharding import PartitionSpec as P

MESH = pl.DeviceIdType.MESH
F32 = jnp.float32
BF16 = jnp.bfloat16
LANES = 128
SIDE = 4
CORES = 2
REACH = 4
EARLY = 4
FIRST = 12
STAGE = 9


def one_hot(mask):
    return jnp.where(mask, 1.0, 0.0).astype(F32).astype(BF16)


def wait_bytes(ref, sem):
    pltpu.make_async_copy(ref, ref, sem).wait()


def iota(shape, axis):
    return lax.broadcasted_iota(jnp.int32, shape, axis)


def kernel(
    groups, peers,
    tiles_hbm, iblock_hbm, jslot_hbm, kslot_hbm, jlist_hbm, klist_hbm, two_hbm, three_hbm,
    out_ref,
    iblock, jslot, kslot, jlist, klist, tiles, table,
    near, asked, order, send, recv, arranged, send_part, recv_part,
    local_sem, tile_sem, near_sem, asked_sem, rows_sem, part_sem, there_sem,
):
    count = iblock.shape[1]
    together = CORES * count
    inner, flat = tiles.shape[1:]
    half = table.shape[1]
    chunks = half // LANES
    slab = 2 * together
    height_two, height_three = two_hbm.shape[0], three_hbm.shape[0]
    planes = peers // SIDE
    me = lax.axis_index("tiles")
    row = lax.axis_index("blk")
    plane, lane_x = me // SIDE, lax.rem(me, SIDE)
    core = lax.rem(row, CORES)
    sibling = row + 1 - 2 * core

    def along(offset):
        return lax.rem(plane + (offset + planes), planes)

    def at_plane(offset):
        return {"tiles": along(offset) * SIDE + lane_x}

    beside = [{"blk": sibling}]
    for step in (2, 1, 3):
        other = plane * SIDE + lax.rem(lane_x + step, SIDE)
        beside += [{"tiles": other}, {"tiles": other, "blk": sibling}]
    owners = [lax.rem(row + step, groups) for step in range(1, groups)]
    close = [sign * away for away in range(REACH, 0, -1) for sign in (1, -1)]
    distant = [planes // 2] + [
        sign * away for away in range(planes // 2 - 1, REACH, -1) for sign in (1, -1)
    ]

    barrier = pltpu.get_barrier_semaphore()
    greeted = [at_plane(offset) for offset in close] + beside
    greeted += [
        {"blk": lax.rem(row + 2 * step + side, groups)}
        for step in range(1, groups // CORES) for side in (0, sibling - row)
    ]
    for target in greeted:
        pl.semaphore_signal(barrier, inc=1, device_id=target, device_id_type=MESH)

    pairs = [
        (iblock_hbm, iblock), (jslot_hbm, jslot), (kslot_hbm, kslot), (jlist_hbm, jlist),
        (klist_hbm, klist),
    ]
    columns = pl.ds(pl.multiple_of(core * half, half), half)
    pairs.append((two_hbm.at[:, columns], table.at[pl.ds(0, height_two)]))
    pairs.append((three_hbm.at[:, columns], table.at[pl.ds(height_two, height_three)]))
    mine = pl.ds(core * count, count)
    pairs.append((tiles_hbm, tiles.at[mine]))
    loads = [
        pltpu.make_async_copy(source, target, local_sem.at[index])
        for index, (source, target) in enumerate(pairs)
    ]
    for load in loads:
        load.start()
    for load in loads[:5]:
        load.wait()
    lane = iota((1, LANES), 1)
    message = jnp.zeros((1, LANES), jnp.int32)
    for which in range(count):
        spot = lane_x * together + core * count + which
        values = (jlist[0, jslot[0, which]], klist[0, kslot[0, which]], iblock[0, which])
        for kind, value in enumerate(values):
            message = jnp.where(lane == kind * SIDE * together + spot, value, message)
    position = pl.ds(lane_x * CORES + core, 1)
    near[position] = message.reshape(1, 1, LANES)

    pl.semaphore_wait(barrier, len(greeted))

    def copy(source, target, send_sem, recv_sem, device):
        pltpu.make_async_remote_copy(
            source, target, send_sem, recv_sem, device_id=device, device_id_type=MESH
        ).start()

    for offset in (REACH, -REACH):
        pl.semaphore_signal(there_sem, inc=1, device_id=at_plane(offset), device_id_type=MESH)
    for target in beside:
        copy(near.at[position], near.at[position], near_sem.at[0], near_sem.at[1], target)
    copy(tiles_hbm, tiles.at[mine], tile_sem.at[0], tile_sem.at[1], beside[0])

    wide = peers * slab
    order[...] = one_hot(
        iota((wide, wide), 1) == (iota((wide, wide), 0) % peers) * slab + iota((wide, wide), 0) // peers
    )

    wait_bytes(near.at[pl.ds(0, len(beside))], near_sem.at[1])
    asked[pl.ds(plane, 1)] = jnp.sum(near[...], axis=0, keepdims=True)

    spare = height_two + height_three
    table[spare:, :] = jnp.zeros((table.shape[0] - spare, half), BF16)

    def pass_on(origin, offset, away):
        entry = asked.at[pl.ds(origin, 1)]
        copy(entry, entry, asked_sem.at[planes], asked_sem.at[away % planes], at_plane(offset))

    for offset in close:
        pass_on(plane, offset, offset)

    @pl.when(plane >= EARLY)
    def _():
        pl.semaphore_wait(there_sem, 2)
        for offset in distant:
            pass_on(plane, offset, offset)

    def arrival(away):
        wait_bytes(asked.at[pl.ds(along(-away), 1)], asked_sem.at[away % planes])

    ahead = jnp.logical_and(plane >= REACH, plane < REACH + EARLY)
    behind = plane >= planes - REACH

    @pl.when(ahead)
    def _():
        arrival(REACH)
        for step in range(1, planes // 2 - REACH + 1):
            pass_on(along(-REACH), step, REACH + step)

    @pl.when(behind)
    def _():
        arrival(-REACH)
        for step in range(1, planes // 2 - REACH):
            pass_on(along(REACH), -step, -REACH - step)

    for load in loads[5:]:
        load.wait()
    rows = SIDE * slab

    def select(origins):
        total = rows * len(origins)
        given = jnp.concatenate(
            [jnp.broadcast_to(asked[origin], (rows, LANES)) for origin in origins], axis=0
        )
        place = iota((total, LANES), 0) % rows
        kind = place % slab // together
        spot = kind * SIDE * together + place // slab * together + place % together
        lane = iota((total, LANES), 1)
        wanted = jnp.sum(jnp.where(lane == spot, given, 0), axis=1, keepdims=True)
        key = wanted + kind * height_two
        hot = jnp.concatenate(
            [one_hot(key == lane + start) for start in range(0, table.shape[0], LANES)], axis=1
        )
        picked = jnp.dot(hot, table[...], preferred_element_type=F32).astype(BF16)
        for index, origin in enumerate(origins):
            for c in range(chunks):
                send[c, pl.ds(origin * SIDE, SIDE)] = picked[
                    index * rows : (index + 1) * rows, c * LANES : (c + 1) * LANES
                ].reshape(SIDE, slab, LANES)

    def give(c, origin, others=(2, 1, 3, 0)):
        for step in others:
            other = origin * SIDE + lax.rem(lane_x + step, SIDE)
            copy(
                send.at[c, other], recv.at[c, me], rows_sem.at[0, c], rows_sem.at[1, c],
                {"tiles": other},
            )

    def serve(origin, away, parts):
        known = jnp.logical_or(
            jnp.logical_and(ahead, away == REACH),
            jnp.logical_and(behind, away == planes - REACH),
        )

        @pl.when(jnp.logical_not(known))
        def _():
            wait_bytes(asked.at[pl.ds(origin, 1)], asked_sem.at[away])

        select([origin])
        for c in parts:
            give(c, origin)

    select([plane])
    for c in range(chunks):
        recv[c, pl.ds(me, 1)] = send[c, pl.ds(me, 1)]
        give(c, plane, (2, 1, 3))
    for origin in range(FIRST):
        away = lax.rem(plane + planes - origin, planes)

        @pl.when(plane != origin)
        def _():
            serve(origin, away, range(chunks))

    def others(offsets, visit):
        for offset in offsets:
            origin = along(-offset)

            @pl.when(origin >= FIRST)
            def _():
                visit(origin, offset % planes)

    others(reversed(close), lambda origin, away: serve(origin, away, range(chunks)))
    others(reversed(distant), lambda origin, away: serve(origin, away, (0,)))
    for c in range(1, chunks):
        others(reversed(distant), lambda origin, away: give(c, origin))

    wait_bytes(near.at[pl.ds(0, len(beside))], near_sem.at[0])
    wait_bytes(asked.at[pl.ds(0, 2 * REACH)], asked_sem.at[planes])

    @pl.when(plane >= EARLY)
    def _():
        wait_bytes(asked.at[pl.ds(0, planes - 1 - 2 * REACH)], asked_sem.at[planes])

    @pl.when(plane < EARLY)
    def _():
        pl.semaphore_wait(there_sem, 2)

    @pl.when(ahead)
    def _():
        wait_bytes(asked.at[pl.ds(0, planes // 2 - REACH)], asked_sem.at[planes])

    @pl.when(behind)
    def _():
        wait_bytes(asked.at[pl.ds(0, planes // 2 - REACH - 1)], asked_sem.at[planes])

    wait_bytes(tiles.at[pl.ds(0, count)], tile_sem.at[1])
    wait_bytes(tiles.at[pl.ds(0, count)], tile_sem.at[0])

    some = pl.ds(0, peers - 1)
    step = 4
    depth = flat // peers
    summary = asked[plane]
    homes = []
    for which in range(together):
        spot = 2 * SIDE * together + lane_x * together + which
        homes.append(jnp.sum(jnp.where(lane == spot, summary, 0), axis=1, keepdims=True))
    for c in range(chunks):
        wait_bytes(recv.at[c, some], rows_sem.at[1, c])
        arranged[...] = jnp.dot(
            order[...], recv[c].reshape(wide, LANES), preferred_element_type=F32
        )
        if STAGE < 5:
            continue
        terms = []
        for which in range(together):
            top = which * peers
            mode_three = arranged[(together + which) * peers : (together + which + 1) * peers, :]
            term = jnp.zeros((inner, LANES), F32)
            for first in range(0, peers, step):
                product = jnp.concatenate(
                    [
                        (mode_three * arranged[top + j : top + j + 1, :]).astype(BF16)
                        for j in range(first, first + step)
                    ],
                    axis=0,
                )
                left = tiles[which, :, first * depth : (first + step) * depth]
                term = term + jnp.dot(left, product, preferred_element_type=F32)
            terms.append(term)
        for group in range(groups):
            total = jnp.zeros((inner, LANES), F32)
            for which in range(together):
                total = total + jnp.where(homes[which] == group, terms[which], 0.0)
            send_part[c, group] = total.astype(BF16)
        if STAGE < 6:
            continue
        for other in owners:
            copy(
                send_part.at[c, other], recv_part.at[c, row], part_sem.at[0, c],
                part_sem.at[1, c], {"blk": other},
            )
        recv_part[c, pl.ds(row, 1)] = send_part[c, pl.ds(row, 1)]
    for c in range(chunks):
        wait_bytes(send.at[c, some], rows_sem.at[0, c])
    if STAGE < 6:
        out_ref[...] = jnp.zeros_like(out_ref)
        return
    for c in range(chunks):
        wait_bytes(recv_part.at[c, pl.ds(0, groups - 1)], part_sem.at[1, c])
        for side in range(CORES):
            total = recv_part[c, side].astype(F32)
            for group in range(side + CORES, groups, CORES):
                total = total + recv_part[c, group].astype(F32)
            start = side * half + c * LANES
            out_ref[:, start : start + LANES] = total
    for c in range(chunks):
        wait_bytes(send_part.at[c, pl.ds(0, groups - 1)], part_sem.at[0, c])


def per_device(
    tensor_tiles, tile_iblock, tile_jslot, tile_kslot, block_jlist, block_klist, factor_b, factor_c
):
    groups = lax.axis_size("blk")
    peers = lax.axis_size("tiles")
    tiles = tensor_tiles[0]
    two = factor_b.reshape(factor_b.shape[0], factor_b.shape[2])
    three = factor_c.reshape(factor_c.shape[0], factor_c.shape[2])
    count, inner, flat = tiles.shape
    together = CORES * count
    rank = two.shape[1]
    half = rank // CORES
    chunks = half // LANES
    slab = 2 * together
    wide = peers * slab
    planes = peers // SIDE
    height = -(-(two.shape[0] + three.shape[0]) // LANES) * LANES
    dma = pltpu.SemaphoreType.DMA
    exchanged = pltpu.VMEM((chunks, peers, slab, LANES), BF16)
    part = pltpu.VMEM((chunks, groups, inner, LANES), BF16)
    return pl.pallas_call(
        functools.partial(kernel, groups, peers),
        out_shape=jax.ShapeDtypeStruct((inner, rank), F32),
        in_specs=[pl.BlockSpec(memory_space=pl.ANY)] * 8,
        out_specs=pl.BlockSpec(memory_space=pltpu.VMEM),
        scratch_shapes=[
            *[pltpu.SMEM((1, count), jnp.int32)] * 5,
            pltpu.VMEM((together, inner, flat), BF16),
            pltpu.VMEM((height, half), BF16),
            pltpu.VMEM((SIDE * CORES, 1, LANES), jnp.int32),
            pltpu.VMEM((planes, 1, LANES), jnp.int32),
            pltpu.VMEM((wide, wide), BF16),
            exchanged, exchanged, pltpu.VMEM((wide, LANES), F32), part, part,
            dma((8,)), dma((2,)), dma((2,)), dma((planes + 1,)), dma((2, chunks)), dma((2, chunks)),
            pltpu.SemaphoreType.REGULAR,
        ],
        compiler_params=pltpu.CompilerParams(collective_id=0, has_side_effects=True),
    )(tiles, tile_iblock, tile_jslot, tile_kslot, block_jlist, block_klist, two, three)


def solution(mesh):
    placed = (
        P("blk", "tiles", None, None),
        P("blk", "tiles"),
        P("blk", "tiles"),
        P("blk", "tiles"),
        P("blk", "tiles"),
        P("blk", "tiles"),
        P(None, "tiles", None),
        P(None, "tiles", None),
    )
    return jax.shard_map(
        per_device, mesh=mesh, in_specs=placed, out_specs=P(("blk", "tiles"), None), check_vma=False
    )
```

time: 148 us -> 45.7 us (0.31)
  waiting for transfers between devices: 62.9 us -> 0 us
  Pallas kernels: 0 us -> 43.9 us
  blocking collectives: 29.6 us -> 0 us
  between operations: 14.2 us -> 0.01 us
  starting transfers between devices: 12.1 us -> 0 us
  local copies, waits for them, and re-layouts: 13 us -> 1.57 us
  loops' own time: 6.83 us -> 0 us
  other arithmetic: 5.82 us -> 0 us
  matrix products: 2.49 us -> 0 us
    pallas_call x0 -> x1, Pallas kernels: none -> 43.9 us  [per_device(): pl.pallas_call(functools.partial(kernel, groups, peers), out_shape=jax.Sh...]
    reduce_scatter x1 -> x0, waiting for transfers between devices: 34.8 us -> none  [per_device(): lax.psum_scatter(rounded.reshape(groups * inner, rank).astype(jnp.bfloat1...]
    unnamed x1 -> x0, blocking collectives: 29.6 us -> none
    all_to_all x2 -> x0, waiting for transfers between devices: 28.1 us -> none  [the longest x1 15.1 us: per_device(): lax.all_to_all(outgoing(asked_two, factor_b, count), 'tiles', split_axis=...]
    all_to_all x2 -> x0, starting transfers between devices: 12.1 us -> none  [the longest x1 7.47 us: per_device(): lax.all_to_all(outgoing(asked_three, factor_c, count), 'tiles', split_axi...]
    another operation x1 -> x0, loops' own time: 6.83 us -> none  [per_device(): lax.fori_loop(0, count, accumulate, jnp.zeros((groups, inner, rank), jnp....]
    dynamic_slice x6 -> x0, local copies, waits for them, and re-layouts: 4.49 us -> none  [the longest x2 2.16 us: tile_term(): tile_block = lax.dynamic_index_in_dim(local_tiles, which, 0, keepdims=False)]
    gather x4 -> x0, local copies, waits for them, and re-layouts: 4.29 us -> none  [the longest x2 1.7 us: outgoing(): return jnp.take(local, table, axis=0)]
  transfers between devices with their start and end apart: 3 -> 0, of which waited for: 3 -> 0; matrix products, arithmetic and copies ran while one was open for 1% -> 0% of each run, Pallas kernels for 0% -> 0%
where the time goes in v3:
time: 45.7 us; the launch traced here: 45.5 us
  Pallas kernels  43.9 us (96%)
  local copies, waits for them, and re-layouts  1.57 us (3%)
    pallas_call x1, Pallas kernels, per_device(): pl.pallas_call(functools.partial(kernel, groups, peers), out_shape=jax.Sh...  43.9 us
    unnamed x1, local copies, waits for them, and re-layouts  1.57 us

profile of v3, /device:TPU:1, one launch (start us, length us, event | category | flops | bytes accessed | tf_op | source)
XLA Modules:
  0.0 45.5 jit_solution(14809438115452507416)
XLA Ops:
  0.0 43.9 %shard_map.82 = f32[64,512]{1,0:T(8,128)} custom-call(bf16[2,64,4096]{2,1,0:T(8,128)(2,1)} %bitcast.3, s32[1,2]{1,0:T(1,128)} %iblock_hbm.1, s32[1,2]{1,0:T(1,128)} %jslot_hbm.1, s32[1,2]{1,0:T(1,128)} %kslot_hbm.1, s32[1,2]{1,0:T(1,128)} %jlist_hbm.1, s32[1,2]{1,0:T(1,128)} %klist_hbm.1, bf16[256,512]{1,0:T(8,128)(2,1)} %bitcast.4, bf16[64,512]{1,0:T(8,128)(2,1)} %bitcast.5), custom_call_target="tpu_custom_call" | custom-call | tf_op jit(solution)/shard_map/pallas_call | solution.py:337
  44.0 1.6 %copy.10 = f32[64,512]{1,0:T(8,128)} copy(f32[64,512]{1,0:T(8,128)} %shard_map.82) | data formatting | bytes 262144

commit v4 on v3

--- a/solution.py
+++ b/solution.py
@@ -14,8 +14,9 @@
 SIDE = 4
 CORES = 2
 REACH = 4
-EARLY = 4
-FIRST = 12
+HOP = 2
+FIRST = 8
+AHEAD = 6
 STAGE = 9
 
 
@@ -37,7 +38,7 @@
     out_ref,
     iblock, jslot, kslot, jlist, klist, tiles, table,
     near, asked, order, send, recv, arranged, send_part, recv_part,
-    local_sem, tile_sem, near_sem, asked_sem, rows_sem, part_sem, there_sem,
+    local_sem, tile_sem, near_sem, asked_sem, rows_sem, part_sem, there_sem, chain_sem,
 ):
     count = iblock.shape[1]
     together = CORES * count
@@ -70,13 +71,32 @@
     ]
 
     barrier = pltpu.get_barrier_semaphore()
-    greeted = [at_plane(offset) for offset in close] + beside
-    greeted += [
+    split = planes // 2
+    late = plane >= split
+
+    def below(offset):
+        return jnp.logical_and(along(offset) < split, along(offset) < plane)
+
+    def above(offset):
+        return jnp.logical_and(plane < split, along(offset) > plane)
+
+    def both_late(offset):
+        return jnp.logical_and(late, along(offset) >= split)
+
+    def signal(sem, target):
+        pl.semaphore_signal(sem, inc=1, device_id=target, device_id_type=MESH)
+
+    for offset in close:
+        told = jnp.logical_and(above(offset), along(offset) < split)
+        if abs(offset) <= HOP:
+            told = jnp.logical_or(told, both_late(offset))
+        pl.when(told)(lambda: signal(barrier, at_plane(offset)))
+    greeted = beside + [
         {"blk": lax.rem(row + 2 * step + side, groups)}
         for step in range(1, groups // CORES) for side in (0, sibling - row)
     ]
     for target in greeted:
-        pl.semaphore_signal(barrier, inc=1, device_id=target, device_id_type=MESH)
+        signal(barrier, target)
 
     pairs = [
         (iblock_hbm, iblock), (jslot_hbm, jslot), (kslot_hbm, kslot), (jlist_hbm, jlist),
@@ -105,15 +125,34 @@
     position = pl.ds(lane_x * CORES + core, 1)
     near[position] = message.reshape(1, 1, LANES)
 
-    pl.semaphore_wait(barrier, len(greeted))
+    expected = len(greeted)
+    for offset in close:
+        due = below(offset)
+        if abs(offset) <= HOP:
+            due = jnp.logical_or(due, both_late(offset))
+        expected = expected + jnp.where(due, 1, 0)
+    pl.semaphore_wait(barrier, expected)
+    for offset in close:
+        told = jnp.logical_and(above(offset), along(offset) >= split)
+        pl.when(told)(lambda: signal(barrier, at_plane(offset)))
 
     def copy(source, target, send_sem, recv_sem, device):
         pltpu.make_async_remote_copy(
             source, target, send_sem, recv_sem, device_id=device, device_id_type=MESH
         ).start()
 
-    for offset in (REACH, -REACH):
-        pl.semaphore_signal(there_sem, inc=1, device_id=at_plane(offset), device_id_type=MESH)
+    def chain(step):
+        for offset in (HOP, -HOP):
+            target = {"tiles": along(offset) * SIDE + lane_x}
+            pl.when(both_late(offset))(lambda: signal(chain_sem.at[step], target))
+
+    def chain_wait(step):
+        links = sum(jnp.where(both_late(offset), 1, 0) for offset in (HOP, -HOP))
+        pl.when(late)(lambda: pl.semaphore_wait(chain_sem.at[step], links))
+
+    chain(0)
+    for offset in close:
+        pl.when(below(offset))(lambda: signal(there_sem.at[-offset % planes], at_plane(offset)))
     for target in beside:
         copy(near.at[position], near.at[position], near_sem.at[0], near_sem.at[1], target)
     copy(tiles_hbm, tiles.at[mine], tile_sem.at[0], tile_sem.at[1], beside[0])
@@ -123,42 +162,60 @@
         iota((wide, wide), 1) == (iota((wide, wide), 0) % peers) * slab + iota((wide, wide), 0) // peers
     )
 
+    spare = height_two + height_three
+    table[spare:, :] = jnp.zeros((table.shape[0] - spare, half), BF16)
+    chain_wait(0)
+    chain(1)
     wait_bytes(near.at[pl.ds(0, len(beside))], near_sem.at[1])
     asked[pl.ds(plane, 1)] = jnp.sum(near[...], axis=0, keepdims=True)
-
-    spare = height_two + height_three
-    table[spare:, :] = jnp.zeros((table.shape[0] - spare, half), BF16)
 
     def pass_on(origin, offset, away):
         entry = asked.at[pl.ds(origin, 1)]
         copy(entry, entry, asked_sem.at[planes], asked_sem.at[away % planes], at_plane(offset))
 
-    for offset in close:
-        pass_on(plane, offset, offset)
-
-    @pl.when(plane >= EARLY)
-    def _():
-        pl.semaphore_wait(there_sem, 2)
-        for offset in distant:
-            pass_on(plane, offset, offset)
-
     def arrival(away):
         wait_bytes(asked.at[pl.ds(along(-away), 1)], asked_sem.at[away % planes])
 
-    ahead = jnp.logical_and(plane >= REACH, plane < REACH + EARLY)
-    behind = plane >= planes - REACH
+    for offset in close:
+        pl.when(jnp.logical_or(late, below(offset)))(lambda: pass_on(plane, offset, offset))
+    for offset in sorted(close, key=lambda offset: offset % planes if offset > 0 else planes - offset):
+        @pl.when(above(offset))
+        def _():
+            pl.semaphore_wait(there_sem.at[offset % planes], 1)
+            pass_on(plane, offset, offset)
+
+    nearer = [offset for offset in distant if abs(offset) <= 3 * HOP]
+    farther = [offset for offset in distant if abs(offset) > 3 * HOP]
+    for step, offsets in ((1, nearer), (2, farther)):
+        chain_wait(step)
+        if step == 1:
+            chain(2)
+
+        @pl.when(late)
+        def _():
+            for offset in offsets:
+                pass_on(plane, offset, offset)
+
+    ahead = jnp.logical_and(plane >= REACH, plane < planes - REACH)
+    behind = jnp.logical_not(ahead)
 
     @pl.when(ahead)
     def _():
         arrival(REACH)
-        for step in range(1, planes // 2 - REACH + 1):
-            pass_on(along(-REACH), step, REACH + step)
+
+        @pl.when(along(-REACH) < split)
+        def _():
+            for step in range(1, AHEAD + 1):
+                pass_on(along(-REACH), step, REACH + step)
 
     @pl.when(behind)
     def _():
         arrival(-REACH)
-        for step in range(1, planes // 2 - REACH):
-            pass_on(along(REACH), -step, -REACH - step)
+
+        @pl.when(along(REACH) < split)
+        def _():
+            for step in range(1, 2 * (split - REACH) - AHEAD):
+                pass_on(along(REACH), -step, -REACH - step)
 
     for load in loads[5:]:
         load.wait()
@@ -226,29 +283,27 @@
             def _():
                 visit(origin, offset % planes)
 
-    others(reversed(close), lambda origin, away: serve(origin, away, range(chunks)))
+    near_first = list(reversed(close))
+    far_first = distant
+    others(near_first, lambda origin, away: serve(origin, away, (0,)))
     others(reversed(distant), lambda origin, away: serve(origin, away, (0,)))
-    for c in range(1, chunks):
-        others(reversed(distant), lambda origin, away: give(c, origin))
+    others(far_first, lambda origin, away: give(1, origin))
+    others(close, lambda origin, away: give(1, origin))
 
     wait_bytes(near.at[pl.ds(0, len(beside))], near_sem.at[0])
     wait_bytes(asked.at[pl.ds(0, 2 * REACH)], asked_sem.at[planes])
 
-    @pl.when(plane >= EARLY)
+    @pl.when(late)
     def _():
         wait_bytes(asked.at[pl.ds(0, planes - 1 - 2 * REACH)], asked_sem.at[planes])
 
-    @pl.when(plane < EARLY)
+    @pl.when(jnp.logical_and(ahead, along(-REACH) < split))
     def _():
-        pl.semaphore_wait(there_sem, 2)
-
-    @pl.when(ahead)
+        wait_bytes(asked.at[pl.ds(0, AHEAD)], asked_sem.at[planes])
+
+    @pl.when(jnp.logical_and(behind, along(REACH) < split))
     def _():
-        wait_bytes(asked.at[pl.ds(0, planes // 2 - REACH)], asked_sem.at[planes])
-
-    @pl.when(behind)
-    def _():
-        wait_bytes(asked.at[pl.ds(0, planes // 2 - REACH - 1)], asked_sem.at[planes])
+        wait_bytes(asked.at[pl.ds(0, 2 * (split - REACH) - AHEAD - 1)], asked_sem.at[planes])
 
     wait_bytes(tiles.at[pl.ds(0, count)], tile_sem.at[1])
     wait_bytes(tiles.at[pl.ds(0, count)], tile_sem.at[0])
@@ -336,7 +391,7 @@
     part = pltpu.VMEM((chunks, groups, inner, LANES), BF16)
     return pl.pallas_call(
         functools.partial(kernel, groups, peers),
-        out_shape=jax.ShapeDtypeStruct((inner, rank), F32),
+        out_shape=pltpu.VMEM((inner, rank), F32),
         in_specs=[pl.BlockSpec(memory_space=pl.ANY)] * 8,
         out_specs=pl.BlockSpec(memory_space=pltpu.VMEM),
         scratch_shapes=[
@@ -348,7 +403,7 @@
             pltpu.VMEM((wide, wide), BF16),
             exchanged, exchanged, pltpu.VMEM((wide, LANES), F32), part, part,
             dma((8,)), dma((2,)), dma((2,)), dma((planes + 1,)), dma((2, chunks)), dma((2, chunks)),
-            pltpu.SemaphoreType.REGULAR,
+            pltpu.SemaphoreType.REGULAR((planes,)), pltpu.SemaphoreType.REGULAR((3,)),
         ],
         compiler_params=pltpu.CompilerParams(collective_id=0, has_side_effects=True),
     )(tiles, tile_iblock, tile_jslot, tile_kslot, block_jlist, block_klist, two, three)

time: 45.7 us -> 42 us (0.919)
  the two profiles are of different devices: /device:TPU:1 before, /device:TPU:289 now
where the time goes in v4:
time: 42 us; the launch traced here: 41.8 us
  Pallas kernels  41.2 us (98%)
  local copies, waits for them, and re-layouts  0.66 us (2%)
    pallas_call x1, Pallas kernels, per_device(): pl.pallas_call(functools.partial(kernel, groups, peers), out_shape=pltpu....  41.2 us

profile of v4, /device:TPU:289, one launch (start us, length us, event | category | flops | bytes accessed | tf_op | source)
XLA Modules:
  0.0 41.8 jit_solution(11188551177896542728)
XLA Ops:
  0.0 41.2 %shard_map.82 = f32[64,512]{1,0:T(8,128)S(1)} custom-call(bf16[2,64,4096]{2,1,0:T(8,128)(2,1)} %bitcast.3, s32[1,2]{1,0:T(1,128)} %iblock_hbm.1, s32[1,2]{1,0:T(1,128)} %jslot_hbm.1, s32[1,2]{1,0:T(1,128)} %kslot_hbm.1, s32[1,2]{1,0:T(1,128)} %jlist_hbm.1, s32[1,2]{1,0:T(1,128)} %klist_hbm.1, bf16[256,512]{1,0:T(8,128)(2,1)} %bitcast.4, bf16[64,512]{1,0:T(8,128)(2,1)} %bitcast.5), custom_call_target="tpu_custom_call" | custom-call | tf_op jit(solution)/shard_map/pallas_call | solution.py:392
  41.2 0.7 %copy.10 = f32[64,512]{1,0:T(8,128)} copy(f32[64,512]{1,0:T(8,128)S(1)} %shard_map.82) | data formatting | bytes 262144

commit v5 on v4

--- a/solution.py
+++ b/solution.py
@@ -17,7 +17,7 @@
 HOP = 2
 FIRST = 8
 AHEAD = 6
-STAGE = 9
+STEP = 4
 
 
 def one_hot(mask):
@@ -184,17 +184,32 @@
             pl.semaphore_wait(there_sem.at[offset % planes], 1)
             pass_on(plane, offset, offset)
 
-    nearer = [offset for offset in distant if abs(offset) <= 3 * HOP]
-    farther = [offset for offset in distant if abs(offset) > 3 * HOP]
-    for step, offsets in ((1, nearer), (2, farther)):
-        chain_wait(step)
-        if step == 1:
-            chain(2)
-
-        @pl.when(late)
-        def _():
-            for offset in offsets:
-                pass_on(plane, offset, offset)
+    def to_early(offset):
+        return along(offset) < split
+
+    def soon(offset):
+        sure = jnp.logical_and(to_early(offset), plane < planes - HOP)
+        if offset == split - 1:
+            sure = jnp.logical_and(sure, plane != split + 1)
+        return sure
+
+    def ask_distant(when):
+        for offset in distant:
+            pl.when(jnp.logical_and(late, when(offset)))(lambda: pass_on(plane, offset, offset))
+
+    ask_distant(soon)
+    chain_wait(1)
+    chain(2)
+    ask_distant(
+        lambda offset: jnp.logical_and(
+            jnp.logical_not(soon(offset)),
+            to_early(offset) if abs(offset) > 3 * HOP else True,
+        )
+    )
+    chain_wait(2)
+    ask_distant(
+        lambda offset: jnp.logical_not(to_early(offset)) if abs(offset) > 3 * HOP else False
+    )
 
     ahead = jnp.logical_and(plane >= REACH, plane < planes - REACH)
     behind = jnp.logical_not(ahead)
@@ -309,7 +324,7 @@
     wait_bytes(tiles.at[pl.ds(0, count)], tile_sem.at[0])
 
     some = pl.ds(0, peers - 1)
-    step = 4
+    step = STEP
     depth = flat // peers
     summary = asked[plane]
     homes = []
@@ -320,43 +335,43 @@
         wait_bytes(recv.at[c, some], rows_sem.at[1, c])
         arranged[...] = jnp.dot(
             order[...], recv[c].reshape(wide, LANES), preferred_element_type=F32
-        )
-        if STAGE < 5:
-            continue
+        ).astype(BF16)
         terms = []
-        for which in range(together):
-            top = which * peers
-            mode_three = arranged[(together + which) * peers : (together + which + 1) * peers, :]
-            term = jnp.zeros((inner, LANES), F32)
+        for pair in range(0, together, 2):
+            both = (pair, pair + 1)
+            term = jnp.zeros((2 * inner, 2 * LANES), F32)
             for first in range(0, peers, step):
                 product = jnp.concatenate(
                     [
-                        (mode_three * arranged[top + j : top + j + 1, :]).astype(BF16)
+                        jnp.concatenate(
+                            [
+                                arranged[(together + which) * peers : (together + which + 1) * peers, :]
+                                * arranged[which * peers + j : which * peers + j + 1, :]
+                                for which in both
+                            ],
+                            axis=1,
+                        )
                         for j in range(first, first + step)
                     ],
                     axis=0,
                 )
-                left = tiles[which, :, first * depth : (first + step) * depth]
+                left = jnp.concatenate(
+                    [tiles[which, :, first * depth : (first + step) * depth] for which in both],
+                    axis=0,
+                )
                 term = term + jnp.dot(left, product, preferred_element_type=F32)
-            terms.append(term)
+            terms += [term[:inner, :LANES], term[inner:, LANES:]]
         for group in range(groups):
             total = jnp.zeros((inner, LANES), F32)
             for which in range(together):
                 total = total + jnp.where(homes[which] == group, terms[which], 0.0)
             send_part[c, group] = total.astype(BF16)
-        if STAGE < 6:
-            continue
         for other in owners:
             copy(
                 send_part.at[c, other], recv_part.at[c, row], part_sem.at[0, c],
                 part_sem.at[1, c], {"blk": other},
             )
         recv_part[c, pl.ds(row, 1)] = send_part[c, pl.ds(row, 1)]
-    for c in range(chunks):
-        wait_bytes(send.at[c, some], rows_sem.at[0, c])
-    if STAGE < 6:
-        out_ref[...] = jnp.zeros_like(out_ref)
-        return
     for c in range(chunks):
         wait_bytes(recv_part.at[c, pl.ds(0, groups - 1)], part_sem.at[1, c])
         for side in range(CORES):
@@ -366,6 +381,7 @@
             start = side * half + c * LANES
             out_ref[:, start : start + LANES] = total
     for c in range(chunks):
+        wait_bytes(send.at[c, some], rows_sem.at[0, c])
         wait_bytes(send_part.at[c, pl.ds(0, groups - 1)], part_sem.at[0, c])
 
 
@@ -401,7 +417,7 @@
             pltpu.VMEM((SIDE * CORES, 1, LANES), jnp.int32),
             pltpu.VMEM((planes, 1, LANES), jnp.int32),
             pltpu.VMEM((wide, wide), BF16),
-            exchanged, exchanged, pltpu.VMEM((wide, LANES), F32), part, part,
+            exchanged, exchanged, pltpu.VMEM((wide, LANES), BF16), part, part,
             dma((8,)), dma((2,)), dma((2,)), dma((planes + 1,)), dma((2, chunks)), dma((2, chunks)),
             pltpu.SemaphoreType.REGULAR((planes,)), pltpu.SemaphoreType.REGULAR((3,)),
         ],

time: 42 us -> 41.4 us (0.986)
  the two profiles are of different devices: /device:TPU:289 before, /device:TPU:1 now
where the time goes in v5:
time: 41.4 us; the launch traced here: 40.6 us
  Pallas kernels  39.9 us (96%)
  local copies, waits for them, and re-layouts  0.66 us (2%)
    pallas_call x1, Pallas kernels, per_device(): pl.pallas_call(functools.partial(kernel, groups, peers), out_shape=pltpu....  39.9 us

profile of v5, /device:TPU:1, one launch (start us, length us, event | category | flops | bytes accessed | tf_op | source)
XLA Modules:
  0.0 40.6 jit_solution(8912052138557507713)
XLA Ops:
  0.0 39.9 %shard_map.82 = f32[64,512]{1,0:T(8,128)S(1)} custom-call(bf16[2,64,4096]{2,1,0:T(8,128)(2,1)} %bitcast.3, s32[1,2]{1,0:T(1,128)} %iblock_hbm.1, s32[1,2]{1,0:T(1,128)} %jslot_hbm.1, s32[1,2]{1,0:T(1,128)} %kslot_hbm.1, s32[1,2]{1,0:T(1,128)} %jlist_hbm.1, s32[1,2]{1,0:T(1,128)} %klist_hbm.1, bf16[256,512]{1,0:T(8,128)(2,1)} %bitcast.4, bf16[64,512]{1,0:T(8,128)(2,1)} %bitcast.5), custom_call_target="tpu_custom_call" | custom-call | tf_op jit(solution)/shard_map/pallas_call | solution.py:408
  39.9 0.7 %copy.10 = f32[64,512]{1,0:T(8,128)} copy(f32[64,512]{1,0:T(8,128)S(1)} %shard_map.82) | data formatting | bytes 262144

commit v6 on v5

--- a/solution.py
+++ b/solution.py
@@ -64,7 +64,7 @@
     for step in (2, 1, 3):
         other = plane * SIDE + lax.rem(lane_x + step, SIDE)
         beside += [{"tiles": other}, {"tiles": other, "blk": sibling}]
-    owners = [lax.rem(row + step, groups) for step in range(1, groups)]
+    owners = [lax.rem(row + step, groups) for step in (4, 5, 3, 2, 6, 7, 1)]
     close = [sign * away for away in range(REACH, 0, -1) for sign in (1, -1)]
     distant = [planes // 2] + [
         sign * away for away in range(planes // 2 - 1, REACH, -1) for sign in (1, -1)
@@ -125,6 +125,11 @@
     position = pl.ds(lane_x * CORES + core, 1)
     near[position] = message.reshape(1, 1, LANES)
 
+    wide = peers * slab
+    order[...] = one_hot(
+        iota((wide, wide), 1) == (iota((wide, wide), 0) % peers) * slab + iota((wide, wide), 0) // peers
+    )
+
     expected = len(greeted)
     for offset in close:
         due = below(offset)
@@ -156,11 +161,6 @@
     for target in beside:
         copy(near.at[position], near.at[position], near_sem.at[0], near_sem.at[1], target)
     copy(tiles_hbm, tiles.at[mine], tile_sem.at[0], tile_sem.at[1], beside[0])
-
-    wide = peers * slab
-    order[...] = one_hot(
-        iota((wide, wide), 1) == (iota((wide, wide), 0) % peers) * slab + iota((wide, wide), 0) // peers
-    )
 
     spare = height_two + height_three
     table[spare:, :] = jnp.zeros((table.shape[0] - spare, half), BF16)
@@ -361,17 +361,19 @@
                 )
                 term = term + jnp.dot(left, product, preferred_element_type=F32)
             terms += [term[:inner, :LANES], term[inner:, LANES:]]
-        for group in range(groups):
+        def partial(group):
             total = jnp.zeros((inner, LANES), F32)
             for which in range(together):
                 total = total + jnp.where(homes[which] == group, terms[which], 0.0)
-            send_part[c, group] = total.astype(BF16)
+            return total.astype(BF16)
+
         for other in owners:
+            send_part[c, pl.ds(other, 1)] = partial(other).reshape(1, inner, LANES)
             copy(
                 send_part.at[c, other], recv_part.at[c, row], part_sem.at[0, c],
                 part_sem.at[1, c], {"blk": other},
             )
-        recv_part[c, pl.ds(row, 1)] = send_part[c, pl.ds(row, 1)]
+        recv_part[c, pl.ds(row, 1)] = partial(row).reshape(1, inner, LANES)
     for c in range(chunks):
         wait_bytes(recv_part.at[c, pl.ds(0, groups - 1)], part_sem.at[1, c])
         for side in range(CORES):

time: 41.4 us -> 41.2 us (level)
  the two profiles are of different devices: /device:TPU:1 before, /device:TPU:64 now
where the time goes in v6:
time: 41.2 us; the launch traced here: 41 us
  Pallas kernels  40.4 us (98%)
  local copies, waits for them, and re-layouts  0.66 us (2%)
    pallas_call x1, Pallas kernels, per_device(): pl.pallas_call(functools.partial(kernel, groups, peers), out_shape=pltpu....  40.4 us

profile of v6, /device:TPU:64, one launch (start us, length us, event | category | flops | bytes accessed | tf_op | source)
XLA Modules:
  0.0 41.0 jit_solution(4038277805443075492)
XLA Ops:
  0.0 40.4 %shard_map.82 = f32[64,512]{1,0:T(8,128)S(1)} custom-call(bf16[2,64,4096]{2,1,0:T(8,128)(2,1)} %bitcast.3, s32[1,2]{1,0:T(1,128)} %iblock_hbm.1, s32[1,2]{1,0:T(1,128)} %jslot_hbm.1, s32[1,2]{1,0:T(1,128)} %kslot_hbm.1, s32[1,2]{1,0:T(1,128)} %jlist_hbm.1, s32[1,2]{1,0:T(1,128)} %klist_hbm.1, bf16[256,512]{1,0:T(8,128)(2,1)} %bitcast.4, bf16[64,512]{1,0:T(8,128)(2,1)} %bitcast.5), custom_call_target="tpu_custom_call" | custom-call | tf_op jit(solution)/shard_map/pallas_call | solution.py:410
  40.4 0.7 %copy.10 = f32[64,512]{1,0:T(8,128)} copy(f32[64,512]{1,0:T(8,128)S(1)} %shard_map.82) | data formatting | bytes 262144

commit v7 on v6

--- a/solution.py
+++ b/solution.py
@@ -15,7 +15,7 @@
 CORES = 2
 REACH = 4
 HOP = 2
-FIRST = 8
+FIRST = 12
 AHEAD = 6
 STEP = 4
 

time: 41.2 us -> 42.1 us (1.022)
  the two profiles are of different devices: /device:TPU:64 before, /device:TPU:65 now
where the time goes in v7:
time: 42.1 us; the launch traced here: 42 us
  Pallas kernels  41.4 us (98%)
  local copies, waits for them, and re-layouts  0.66 us (2%)
    pallas_call x1, Pallas kernels, per_device(): pl.pallas_call(functools.partial(kernel, groups, peers), out_shape=pltpu....  41.4 us

profile of v7, /device:TPU:65, one launch (start us, length us, event | category | flops | bytes accessed | tf_op | source)
XLA Modules:
  0.0 42.0 jit_solution(16480585718690051983)
XLA Ops:
  0.0 41.4 %shard_map.82 = f32[64,512]{1,0:T(8,128)S(1)} custom-call(bf16[2,64,4096]{2,1,0:T(8,128)(2,1)} %bitcast.3, s32[1,2]{1,0:T(1,128)} %iblock_hbm.1, s32[1,2]{1,0:T(1,128)} %jslot_hbm.1, s32[1,2]{1,0:T(1,128)} %kslot_hbm.1, s32[1,2]{1,0:T(1,128)} %jlist_hbm.1, s32[1,2]{1,0:T(1,128)} %klist_hbm.1, bf16[256,512]{1,0:T(8,128)(2,1)} %bitcast.4, bf16[64,512]{1,0:T(8,128)(2,1)} %bitcast.5), custom_call_target="tpu_custom_call" | custom-call | tf_op jit(solution)/shard_map/pallas_call | solution.py:410
  41.4 0.7 %copy.10 = f32[64,512]{1,0:T(8,128)} copy(f32[64,512]{1,0:T(8,128)S(1)} %shard_map.82) | data formatting | bytes 262144
